TPU v7x, 32 devices: a whole 2x2x4 slice. The times are simulated.
32 devices in a mesh: gx: 2 (over x), yz: 16 (over z, y, core).
Axes of the slice: x: 2, y: 2, z: 4, core: 2. Of those that a mesh axis runs over, the one named last changes fastest.
Arguments:
- system_source_term: float32 [320, 4096], P(None, ('gx', 'yz')), may hold values from -200 to 200
- mass_plus_source: float32 [320, 4096], P(None, ('gx', 'yz')), may hold values from 1 to 4
- lifted_upwind_coupling: float32 [480, 4096], P(None, ('gx', 'yz')), may hold values from 0.5 to 2
- frozen_direction_derivative: float32 [75, 4096], P(None, ('gx', 'yz')), may hold values from -3 to 3
- first_solve_matrix: float32 [320, 320], replicated, may hold values from -0.3125 to 0.3125
- final_solve_matrix: float32 [320, 320], replicated, may hold values from -0.3125 to 0.3125
- middle_cell_matrices: float32 [320, 4096], P(None, ('gx', 'yz')), may hold values from 0.3 to 3
- adjacent_table_slots: int32 [6, 4096], P(None, ('gx', 'yz')), may hold values from 0 to 1264, as said below
- plane_outgoing_cells: int32 [32, 2, 16], P(('gx', 'yz')), may hold values from 0 to 127
- band_outgoing_cells: int32 [32, 2, 16], P(('gx', 'yz')), may hold values from 0 to 127
- small_side_table_slot: int32 [32, 352], P(('gx', 'yz')), may hold values from 0 to 768, as said below
- proprietor_mortar_index: int32 [32, 352], P(('gx', 'yz')), may hold values from 0 to 80, as said below
- outgoing_quadrant_index: int32 [32, 352], P(('gx', 'yz')), may hold values from 0 to 3, as said below
- incoming_mortar_index: int32 [32, 352], P(('gx', 'yz')), may hold values from 0 to 80
- incoming_quadrant_index: int32 [32, 352], P(('gx', 'yz')), may hold values from 0 to 3, as said below
- coarse_mortar_table_slot: int32 [32, 80], P(('gx', 'yz')), may hold values from 0 to 767
Outputs:
- newton_update: float32 [320, 4096], P(None, ('gx', 'yz'))
Inputs may be any that keep to these rules, and one draw needn't show every extreme that they name: `adjacent_table_slots`: column of the neighbour trace in the device's table; 1264 marks a boundary face. `small_side_table_slot`: 768 marks an empty slot, exactly where proprietor_mortar_index is 80. Send slot (m, c) of device (g, k) and receive slot (k, c) of device (g, m) hold the same tile: there proprietor_mortar_index, outgoing_quadrant_index equal incoming_mortar_index, incoming_quadrant_index here; 80 marks an empty slot; no position of an owner's hanging face is sent twice; the live hanging faces of an owner are its first ones; from one device to one owner go at most 22 tiles, a bound reached in every draw; in each gx plane one owner receives 4 * 80 tiles. `outgoing_quadrant_index`: 0 in empty slots. `incoming_quadrant_index`: 0 in empty slots.
All inputs are finite; a program needn't handle non-finite values.
Results may differ from a plain program's by a relative error of at most 0.0003.
Values sent between devices are 32-bit elements; how exact they have to be, the bound alone decides.
No kernel may reach another device: no remote copies, remote signals or barrier semaphores. Data moves between devices by JAX's collectives and lax.ppermute only.
A program may use at most 64 MiB of HBM per device.

v0:
```python
import jax
import jax.numpy as jnp
import numpy as np
from jax import lax
from jax.sharding import PartitionSpec as P

ITERS = 2
maximum_depth = lax.Precision.HIGHEST
epsilon = 1e-06


def with_halo(shard, sides, width, wrap):
    for axis, dim in sides:
        size, length = (lax.axis_size(axis), shard.shape[dim])
        up = [(i, (i + 1) % size) for i in range(size if wrap else size - 1)]
        down = [(j, i) for i, j in up]
        last = lax.slice_in_dim(shard, length - width, length, axis=dim)
        leading = lax.slice_in_dim(shard, 0, width, axis=dim)
        before = lax.ppermute(last, axis, up)
        after = lax.ppermute(leading, axis, down)
        shard = jnp.concatenate([before, shard, after], axis=dim)
    return shard


def gll_tables():
    inv_root = 1.0 / np.sqrt(5.0)
    gll_points = np.array([-1.0, -inv_root, inv_root, 1.0])
    weights = np.array([1.0, 5.0, 5.0, 1.0]) / 6.0

    def lagrange(points):
        values_at = np.ones((len(points), 4))
        for table_slot_index in range(4):
            for m in range(4):
                if m != table_slot_index:
                    values_at[:, table_slot_index] = (
                        values_at[:, table_slot_index]
                        * (points - gll_points[m])
                        / (gll_points[table_slot_index] - gll_points[m])
                    )
        return values_at

    derivative = np.zeros((4, 4))
    for i in range(4):
        for table_slot_index in range(4):
            summed = 0.0
            for m in range(4):
                if m != table_slot_index:
                    product_term = 1.0 / (gll_points[table_slot_index] - gll_points[m])
                    for n in range(4):
                        if n != table_slot_index and n != m:
                            product_term = (
                                product_term
                                * (gll_points[i] - gll_points[n])
                                / (gll_points[table_slot_index] - gll_points[n])
                            )
                    summed = summed + product_term
            derivative[i, table_slot_index] = summed
    halves = [lagrange((gll_points - 1.0) / 2.0), lagrange((gll_points + 1.0) / 2.0)]
    half_projections = [
        0.5 * (1.0 / weights)[:, None] * halve.T * weights[None, :] for halve in halves
    ]
    interpolate = np.stack([np.kron(halves[q // 2], halves[q % 2]) for q in range(4)])
    projection = np.stack(
        [np.kron(half_projections[q // 2], half_projections[q % 2]) for q in range(4)]
    )
    identity_four = np.eye(4)
    node_derivative = np.stack(
        [
            np.kron(derivative, np.kron(identity_four, identity_four)),
            np.kron(identity_four, np.kron(derivative, identity_four)),
            np.kron(identity_four, np.kron(identity_four, derivative)),
        ]
    )
    selection = np.zeros((6, 16, 64))
    for face_id in range(6):
        direction = face_id // 2
        fixed_node = 0 if face_id % 2 == 0 else 3
        for first in range(4):
            for second in range(4):
                if direction == 0:
                    node = fixed_node * 16 + first * 4 + second
                elif direction == 1:
                    node = first * 16 + fixed_node * 4 + second
                else:
                    node = first * 16 + second * 4 + fixed_node
                selection[face_id, first * 4 + second, node] = 1.0
    lifting = selection.transpose(2, 0, 1)
    return (
        jnp.asarray(node_derivative, jnp.float32),
        jnp.asarray(interpolate, jnp.float32),
        jnp.asarray(projection, jnp.float32),
        jnp.asarray(selection, jnp.float32),
        jnp.asarray(lifting, jnp.float32),
    )


def own_traces(argument_array, selection):
    local_count = argument_array.shape[1]
    nodal_view = argument_array.reshape(5, 64, local_count)
    faces = jnp.einsum("fsn,ane->asfe", selection, nodal_view, precision=maximum_depth)
    return faces.reshape(80, 6 * local_count)


def jacobian(
    argument_array,
    own_faces,
    near_faces,
    mass_plus_source,
    lifted_upwind_coupling,
    frozen_direction_derivative,
    node_derivative,
    lifting,
):
    local_count = argument_array.shape[1]
    nodal_view = argument_array.reshape(5, 64, local_count)
    flux_blocks = frozen_direction_derivative.reshape(3, 5, 5, local_count)
    flux_terms = jnp.einsum("dabe,bne->dane", flux_blocks, nodal_view, precision=maximum_depth)
    derived = jnp.einsum("dmn,dane->ame", node_derivative, flux_terms, precision=maximum_depth)
    difference = (own_faces - near_faces).reshape(5, 16, 6, local_count)
    coupling = lifted_upwind_coupling.reshape(6, 5, 16, local_count)
    lifted = jnp.einsum(
        "nfs,fase,asfe->ane", lifting, coupling, difference, precision=maximum_depth
    )
    return mass_plus_source * argument_array + (derived + lifted).reshape(320, local_count)


def solve_cell_system(argument_array, first_solve_matrix, final_solve_matrix, middle_cell_matrices):
    interior_share = jnp.dot(
        first_solve_matrix,
        argument_array,
        precision=maximum_depth,
        preferred_element_type=jnp.float32,
    )
    return jnp.dot(
        final_solve_matrix,
        middle_cell_matrices * interior_share,
        precision=maximum_depth,
        preferred_element_type=jnp.float32,
    )


def mortar_sums(received, incoming_mortar_index, incoming_quadrant_index, projection, hang_count):
    slot_count = received.shape[1]
    face_values = received.reshape(5, 16, slot_count)
    candidates = jnp.einsum("qmn,anc->qamc", projection, face_values, precision=maximum_depth)
    selector_q = (
        incoming_quadrant_index[None, :] == jnp.arange(4, dtype=jnp.int32)[:, None]
    ).astype(jnp.float32)
    projected = jnp.sum(candidates * selector_q[:, None, None, :], axis=0).reshape(80, slot_count)
    onehot = (
        incoming_mortar_index[:, None] == jnp.arange(hang_count, dtype=jnp.int32)[None, :]
    ).astype(jnp.float32)
    return jnp.dot(projected, onehot, precision=maximum_depth, preferred_element_type=jnp.float32)


def fine_replies(coarse_cols, outgoing_quadrant_index, interpolate):
    slot_count = coarse_cols.shape[1]
    face_values = coarse_cols.reshape(5, 16, slot_count)
    candidates = jnp.einsum("qmn,anc->qamc", interpolate, face_values, precision=maximum_depth)
    selector_q = (
        outgoing_quadrant_index[None, :] == jnp.arange(4, dtype=jnp.int32)[:, None]
    ).astype(jnp.float32)
    return jnp.sum(candidates * selector_q[:, None, None, :], axis=0).reshape(80, slot_count)


def least_squares(beta_norm, columns):
    steps_count = len(columns)
    zero_value = jnp.zeros((), jnp.float32)
    target = [beta_norm] + [zero_value] * steps_count
    rotations = []
    upper_rows = []
    for table_slot_index in range(steps_count):
        column = list(columns[table_slot_index])
        for i in range(len(rotations)):
            cos_value, sine_value = rotations[i]
            first_new = cos_value * column[i] + sine_value * column[i + 1]
            second = cos_value * column[i + 1] - sine_value * column[i]
            column[i] = first_new
            column[i + 1] = second
        radius = jnp.sqrt(
            column[table_slot_index] * column[table_slot_index]
            + column[table_slot_index + 1] * column[table_slot_index + 1]
        )
        cos_value = column[table_slot_index] / radius
        sine_value = column[table_slot_index + 1] / radius
        column[table_slot_index] = radius
        rotations.append((cos_value, sine_value))
        target[table_slot_index + 1] = -sine_value * target[table_slot_index]
        target[table_slot_index] = cos_value * target[table_slot_index]
        upper_rows.append(column[: table_slot_index + 1])
    coeffs = [zero_value] * steps_count
    for table_slot_index in reversed(range(steps_count)):
        running = target[table_slot_index]
        for k in range(table_slot_index + 1, steps_count):
            running = running - upper_rows[k][table_slot_index] * coeffs[k]
        coeffs[table_slot_index] = running / upper_rows[table_slot_index][table_slot_index]
    return coeffs


def merged_global(partial_values):
    return lax.psum(partial_values, ("gx", "yz"))


def on_device(
    system_source_term,
    mass_plus_source,
    lifted_upwind_coupling,
    frozen_direction_derivative,
    first_solve_matrix,
    final_solve_matrix,
    middle_cell_matrices,
    adjacent_table_slots,
    plane_outgoing_cells,
    band_outgoing_cells,
    small_side_table_slot,
    proprietor_mortar_index,
    outgoing_quadrant_index,
    incoming_mortar_index,
    incoming_quadrant_index,
    coarse_mortar_table_slot,
):
    node_derivative, interpolate, projection, selection, lifting = gll_tables()
    local_count = system_source_term.shape[1]
    hang_count = coarse_mortar_table_slot.shape[1]
    halo_width = plane_outgoing_cells.shape[2]
    near_index = adjacent_table_slots.reshape(-1)
    defect_array = solve_cell_system(
        system_source_term, first_solve_matrix, final_solve_matrix, middle_cell_matrices
    )
    beta_norm = jnp.sqrt(
        merged_global(jnp.stack([jnp.sum(defect_array * defect_array)]))[0] + epsilon
    )
    arnoldi_directions = [defect_array / beta_norm]
    columns = []
    for table_slot_index in range(ITERS):
        argument_array = arnoldi_directions[table_slot_index]
        own_faces = own_traces(argument_array, selection)
        slab_buffer = jnp.stack(
            [
                jnp.take(own_faces, plane_outgoing_cells[0, 0], axis=1),
                jnp.take(own_faces, local_count + plane_outgoing_cells[0, 1], axis=1),
            ]
        ).reshape(2, 80 * halo_width)
        slab_padded = with_halo(slab_buffer, (("gx", 0),), 1, False)
        side_buffer = jnp.stack(
            [
                jnp.take(own_faces, 2 * local_count + band_outgoing_cells[0, 0], axis=1),
                jnp.take(own_faces, 3 * local_count + band_outgoing_cells[0, 1], axis=1),
            ]
        ).reshape(2, 80 * halo_width)
        side_padded = with_halo(side_buffer, (("yz", 0),), 1, True)
        fine_send = jnp.take(
            own_faces, small_side_table_slot[0], axis=1, mode="fill", fill_value=0.0
        )
        coarse = jnp.take(own_faces, coarse_mortar_table_slot[0], axis=1)
        outgoing = jnp.take(coarse, incoming_mortar_index[0], axis=1, mode="fill", fill_value=0.0)
        fine_recv = lax.all_to_all(fine_send, "yz", split_axis=1, concat_axis=1, tiled=True)
        coarse_cols = lax.all_to_all(outgoing, "yz", split_axis=1, concat_axis=1, tiled=True)
        hang_sum = mortar_sums(
            fine_recv, incoming_mortar_index[0], incoming_quadrant_index[0], projection, hang_count
        )
        replies = fine_replies(coarse_cols, outgoing_quadrant_index[0], interpolate)
        trace_table = jnp.concatenate(
            [
                own_faces,
                slab_padded[0].reshape(80, halo_width),
                slab_padded[3].reshape(80, halo_width),
                side_padded[0].reshape(80, halo_width),
                side_padded[3].reshape(80, halo_width),
                hang_sum,
                replies,
            ],
            axis=1,
        )
        near_faces = jnp.take(trace_table, near_index, axis=1, mode="fill", fill_value=0.0)
        scratch_storage = solve_cell_system(
            jacobian(
                argument_array,
                own_faces,
                near_faces,
                mass_plus_source,
                lifted_upwind_coupling,
                frozen_direction_derivative,
                node_derivative,
                lifting,
            ),
            first_solve_matrix,
            final_solve_matrix,
            middle_cell_matrices,
        )
        column = []
        locals_list = [
            jnp.sum(scratch_storage * arnoldi_directions[i]) for i in range(table_slot_index + 1)
        ] + [jnp.sum(scratch_storage * scratch_storage)]
        totals = merged_global(jnp.stack(locals_list))
        squared = totals[table_slot_index + 1]
        for i in range(table_slot_index + 1):
            coefficient = totals[i]
            scratch_storage = scratch_storage - coefficient * arnoldi_directions[i]
            squared = squared - coefficient * coefficient
            column.append(coefficient)
        new_norm = jnp.sqrt(squared + epsilon)
        column.append(new_norm)
        columns.append(column)
        arnoldi_directions.append(scratch_storage / new_norm)
    coeffs = least_squares(beta_norm, columns)
    newton_update = coeffs[0] * arnoldi_directions[0]
    table_slot_index = 1
    newton_update = newton_update + coeffs[table_slot_index] * arnoldi_directions[table_slot_index]
    return newton_update


def solution(mesh):
    return jax.shard_map(
        on_device,
        mesh=mesh,
        in_specs=(
            P(None, ("gx", "yz")),
            P(None, ("gx", "yz")),
            P(None, ("gx", "yz")),
            P(None, ("gx", "yz")),
            P(),
            P(),
            P(None, ("gx", "yz")),
            P(None, ("gx", "yz")),
            P(("gx", "yz"), None, None),
            P(("gx", "yz"), None, None),
            P(("gx", "yz"), None),
            P(("gx", "yz"), None),
            P(("gx", "yz"), None),
            P(("gx", "yz"), None),
            P(("gx", "yz"), None),
            P(("gx", "yz"), None),
        ),
        out_specs=P(None, ("gx", "yz")),
        check_vma=False,
    )
```

profile of v0, /device:TPU:14, one launch (start us, length us, event | category | flops | bytes accessed | tf_op | source)
XLA Modules:
  0.0 263.6 jit_solution(4759819469362136421)
XLA Ops:
  0.0 1.0 copy-done
  1.0 1.5 convolution_multiply_fusion
  2.6 2.2 multiply_reduce_fusion.3
  4.8 40.6 %psum.21 = f32[1]{0:T(128)} all-reduce(f32[1]{0:T(128)} %bitcast), channel_id=1, replica_groups=mesh['gx'=2,'yz'=16] {'gx','yz'}, use_global_device_ids=true, to_apply=%region_1.0 | all-reduce | flops 1 | bytes 8 | tf_op jit(solution)/shard_map/psum | solution.py:201
  48.4 1.3 collective-permute-start
  51.1 4.5 %collective-permute-start.1 = (f32[1,1280]{1,0:T(1,128)}, f32[1,1280]{1,0:T(1,128)S(1)}, u32[]{:S(2)}, u32[]{:S(2)}) collective-permute-start(f32[1,1280]{1,0:T(1,128)} %slice.66), channel_id=1, source_target_pairs={{16,0},{17,1},{18,2},{19,3},{20,4},{21,5},{22,6},{23,7},{24,8},{25... | collective-permute-start | bytes 15368 | tf_op jit(solution)/shard_map/ppermute | solution.py:20
  58.6 1.7 collective-permute-start.3
  61.0 1.1 gather_fusion.4
  62.2 0.7 all_to_all.24
  62.9 7.9 %all-to-all-start = ((f32[80,16,22]{0,2,1:T(8,128)}), f32[80,16,22]{0,2,1:T(8,128)}, u32[]{:S(2)}, u32[]{:S(2)}) async-start(f32[80,16,22]{0,2,1:T(8,128)} %all_to_all.24), calls=%async_computation | async-start | bytes 393216 | tf_op jit(solution)/shard_map/all_to_all | solution.py:257
  73.2 1.0 copy.180
  76.8 3.7 %convolution_bitcast_fusion.1 = f32[3,5,64,128]{2,1,0,3:T(8,128)S(1)} fusion(f32[5,64,128,1]{1,0,3,2:T(8,128)} %copy.180, f32[3,5,5,128]{2,1,0,3:T(8,128)S(1)} %copy.130), kind=kOutput, calls=%fused_computation.17 | convolution fusion | flops 7372800 | bytes 693760 | tf_op jit(solution)/shard_map/dabe,bne->dane/dot_general | solution.py:117
  80.5 2.0 convolution_bitcast_fusion.13
  82.5 1.1 gather_fusion.6
  85.8 6.1 %all-to-all-start.1 = ((f32[80,16,22]{0,2,1:T(8,128)}), f32[80,16,22]{0,2,1:T(8,128)S(1)}, u32[]{:S(2)}, u32[]{:S(2)}) async-start(f32[80,16,22]{0,2,1:T(8,128)} %all_to_all.26), calls=%async_computation.1 | async-start | bytes 393216 | tf_op jit(solution)/shard_map/all_to_all | solution.py:258
  91.9 2.1 copy.142
  94.0 1.4 reshape.366
  95.3 2.4 all-to-all-done.1
  97.8 1.2 copy.144
  98.9 1.4 reshape.368
  101.0 1.3 fusion.4
  102.3 1.1 convolution_dynamic-update-slice_fusion.1
  103.4 2.6 gather_fusion.7
  106.0 1.2 copy.152
  107.2 0.8 bitcast_subtract_fusion.1
  107.9 1.0 reshape.174
  109.0 1.1 bitcast_multiply_fusion.1
  110.1 1.3 fusion.10
  112.0 1.2 fusion.17
  113.2 1.3 pad_maximum_fusion
  114.5 41.6 %psum.22 = f32[2]{0:T(128)S(1)} all-reduce(f32[2]{0:T(128)S(1)} %pad_maximum_fusion), channel_id=1, replica_groups=mesh['gx'=2,'yz'=16] {'gx','yz'}, use_global_device_ids=true, to_apply=%region_6.12 | all-reduce | flops 2 | bytes 16 | tf_op jit(solution)/shard_map/psum | solution.py:201
  163.5 1.6 gather_fusion.12
  165.1 0.7 gather_fusion.13
  166.6 1.0 copy.187
  167.6 3.7 %convolution_bitcast_fusion = f32[3,5,64,128]{2,1,0,3:T(8,128)S(1)} fusion(f32[5,64,128,1]{1,0,3,2:T(8,128)} %copy.187, f32[3,5,5,128]{2,1,0,3:T(8,128)S(1)} %copy.130), kind=kOutput, calls=%fused_computation.16 | convolution fusion | flops 7372800 | bytes 693760 | tf_op jit(solution)/shard_map/dabe,bne->dane/dot_general | solution.py:117
  171.3 1.3 convolution_bitcast_fusion.10
  172.9 1.3 collective-permute-start.4
  174.4 4.5 %collective-permute-start.5 = (f32[1,1280]{1,0:T(1,128)S(1)}, f32[1,1280]{1,0:T(1,128)S(1)}, u32[]{:S(2)}, u32[]{:S(2)}) collective-permute-start(f32[1,1280]{1,0:T(1,128)S(1)} %slice.74), channel_id=1, source_target_pairs={{16,0},{17,1},{18,2},{19,3},{20,4},{21,5},{22,6},{23,7},{24,8},{25... | collective-permute-start | bytes 15368 | tf_op jit(solution)/shard_map/ppermute | solution.py:20
  179.5 1.8 collective-permute-start.7
  182.1 5.9 %all-to-all-start.2 = ((f32[80,16,22]{0,2,1:T(8,128)}), f32[80,16,22]{0,2,1:T(8,128)S(1)}, u32[]{:S(2)}, u32[]{:S(2)}) async-start(f32[80,16,22]{0,2,1:T(8,128)} %all_to_all.28), calls=%async_computation.2 | async-start | bytes 393216 | tf_op jit(solution)/shard_map/all_to_all | solution.py:257
  188.0 1.1 gather_fusion.14
  190.7 3.1 %all-to-all-done.2 = f32[80,16,22]{0,2,1:T(8,128)S(1)} async-done(((f32[80,16,22]{0,2,1:T(8,128)}), f32[80,16,22]{0,2,1:T(8,128)S(1)}, u32[]{:S(2)}, u32[]{:S(2)}) %all-to-all-start.2) | async-done | bytes 112672 | tf_op jit(solution)/shard_map/all_to_all | solution.py:257
  193.8 6.6 %all-to-all-start.3 = ((f32[80,16,22]{0,2,1:T(8,128)}), f32[80,16,22]{0,2,1:T(8,128)S(1)}, u32[]{:S(2)}, u32[]{:S(2)}) async-start(f32[80,16,22]{0,2,1:T(8,128)} %all_to_all.30), calls=%async_computation.3 | async-start | bytes 393216 | tf_op jit(solution)/shard_map/all_to_all | solution.py:258
  201.6 4.6 %all-to-all-done.3 = f32[80,16,22]{0,2,1:T(8,128)S(1)} async-done(((f32[80,16,22]{0,2,1:T(8,128)}), f32[80,16,22]{0,2,1:T(8,128)S(1)}, u32[]{:S(2)}, u32[]{:S(2)}) %all-to-all-start.3) | async-done | bytes 112672 | tf_op jit(solution)/shard_map/all_to_all | solution.py:258
  208.1 1.6 gather_fusion.15
  211.4 1.2 fusion.20
  212.7 2.0 pad_maximum_fusion.1
  214.6 41.7 %psum.23 = f32[3]{0:T(128)S(1)} all-reduce(f32[3]{0:T(128)S(1)} %pad_maximum_fusion.1), channel_id=1, replica_groups=mesh['gx'=2,'yz'=16] {'gx','yz'}, use_global_device_ids=true, to_apply=%region_12.18 | all-reduce | flops 3 | bytes 24 | tf_op jit(solution)/shard_map/psum | solution.py:201
  (266 shorter events, 30.1 us)
Async XLA Ops:
  0.0 46.1 %copy-start.19 = (f32[6,16,64,1]{2,1,0,3:T(8,128)S(1)}, f32[6,16,64,1]{2,1,0,3:T(8,128)}, u32[]{:S(2)}) copy-start(f32[6,16,64,1]{2,1,0,3:T(8,128)} %constant.85) | copy-start | bytes 73732
  2.6 44.9 %copy-start.58 = (s32[1,2,16]{2,1,0:T(2,128)S(1)}, s32[1,2,16]{2,1,0:T(2,128)}, u32[]{:S(2)}) copy-start(s32[1,2,16]{2,1,0:T(2,128)} %param.39) | copy-start | bytes 388
  46.1 65.9 %copy-start.3 = (f32[128,320]{0,1:T(8,128)}, f32[128,320]{0,1:T(8,128)S(1)}, u32[]{:S(2)}) copy-start(f32[128,320]{0,1:T(8,128)S(1)} %broadcast_divide_fusion) | copy-start | bytes 491524
  46.1 9.5 %copy-start.59 = (s32[1,2,16]{2,1,0:T(2,128)S(1)}, s32[1,2,16]{2,1,0:T(2,128)}, u32[]{:S(2)}) copy-start(s32[1,2,16]{2,1,0:T(2,128)} %param.40) | copy-start | bytes 388
  46.6 13.8 %copy-start.54 = (s32[1,352]{1,0:T(1,128)S(1)}, s32[1,352]{1,0:T(1,128)}, u32[]{:S(2)}) copy-start(s32[1,352]{1,0:T(1,128)} %param.41) | copy-start | bytes 4228
  48.4 36.7 %collective-permute-start = (f32[1,1280]{1,0:T(1,128)S(1)}, f32[1,1280]{1,0:T(1,128)S(1)}, u32[]{:S(2)}, u32[]{:S(2)}) collective-permute-start(f32[1,1280]{1,0:T(1,128)S(1)} %slice.64), channel_id=1, source_target_pairs={{0,16},{1,17},{2,18},{3,19},{4,20},{5,21},{6,22},{7,23},{8,24},{9,... | collective-permute-start | bytes 15368 | tf_op jit(solution)/shard_map/ppermute | solution.py:19
  51.1 34.1 %collective-permute-start.1 = (f32[1,1280]{1,0:T(1,128)}, f32[1,1280]{1,0:T(1,128)S(1)}, u32[]{:S(2)}, u32[]{:S(2)}) collective-permute-start(f32[1,1280]{1,0:T(1,128)} %slice.66), channel_id=1, source_target_pairs={{16,0},{17,1},{18,2},{19,3},{20,4},{21,5},{22,6},{23,7},{24,8},{25... | collective-permute-start | bytes 15368 | tf_op jit(solution)/shard_map/ppermute | solution.py:20
  57.2 28.2 %collective-permute-start.2 = (f32[1,1280]{1,0:T(1,128)}, f32[1,1280]{1,0:T(1,128)S(1)}, u32[]{:S(2)}, u32[]{:S(2)}) collective-permute-start(f32[1,1280]{1,0:T(1,128)} %slice.68), channel_id=1, source_target_pairs={{0,1},{1,2},{2,3},{3,4},{4,5},{5,6},{6,7},{7,8},{8,9},{9,10},{10,1... | collective-permute-start | bytes 15368 | tf_op jit(solution)/shard_map/ppermute | solution.py:19
  57.8 13.1 %copy-start.60 = (s32[1,80]{1,0:T(1,128)S(1)}, s32[1,80]{1,0:T(1,128)}, u32[]{:S(2)}) copy-start(s32[1,80]{1,0:T(1,128)} %param.45) | copy-start | bytes 964
  57.8 14.2 %copy-start.55 = (s32[1,352]{1,0:T(1,128)S(1)}, s32[1,352]{1,0:T(1,128)}, u32[]{:S(2)}) copy-start(s32[1,352]{1,0:T(1,128)} %param.43) | copy-start | bytes 4228
  57.8 14.8 %copy-start.33 = (s32[6,128]{1,0:T(8,128)S(1)}, s32[6,128]{1,0:T(8,128)}, u32[]{:S(2)}) copy-start(s32[6,128]{1,0:T(8,128)} %param.38) | copy-start | bytes 9220
  58.6 27.0 %collective-permute-start.3 = (f32[1,1280]{1,0:T(1,128)}, f32[1,1280]{1,0:T(1,128)S(1)}, u32[]{:S(2)}, u32[]{:S(2)}) collective-permute-start(f32[1,1280]{1,0:T(1,128)} %slice.70), channel_id=1, source_target_pairs={{1,0},{2,1},{3,2},{4,3},{5,4},{6,5},{7,6},{8,7},{9,8},{10,9},{11,1... | collective-permute-start | bytes 15368 | tf_op jit(solution)/shard_map/ppermute | solution.py:20
  60.4 12.8 %copy-start.40 = (pred[352]{0:T(512)(128)(4,1)}, pred[352]{0:T(512)(128)(4,1)S(1)}, u32[]{:S(2)}) copy-start(pred[352]{0:T(512)(128)(4,1)S(1)} %compare_and_fusion.3) | copy-start | bytes 1060
  62.1 12.1 %copy-start.27 = (f32[75,128]{1,0:T(8,128)S(1)}, f32[75,128]{1,0:T(8,128)}, u32[]{:S(2)}) copy-start(f32[75,128]{1,0:T(8,128)} %param.34) | copy-start | bytes 115204
  62.9 22.8 %all-to-all-start = ((f32[80,16,22]{0,2,1:T(8,128)}), f32[80,16,22]{0,2,1:T(8,128)}, u32[]{:S(2)}, u32[]{:S(2)}) async-start(f32[80,16,22]{0,2,1:T(8,128)} %all_to_all.24), calls=%async_computation | async-start | bytes 393216 | tf_op jit(solution)/shard_map/all_to_all | solution.py:257
  70.8 4.0 %copy-start.56 = (s32[1,352]{1,0:T(1,128)S(1)}, s32[1,352]{1,0:T(1,128)}, u32[]{:S(2)}) copy-start(s32[1,352]{1,0:T(1,128)} %param.44) | copy-start | bytes 4228
  70.8 4.6 %copy-start.57 = (s32[1,352]{1,0:T(1,128)S(1)}, s32[1,352]{1,0:T(1,128)}, u32[]{:S(2)}) copy-start(s32[1,352]{1,0:T(1,128)} %param.42) | copy-start | bytes 4228
  76.1 4.3 %copy-start.39 = (s32[1024]{0:T(1024)}, s32[1024]{0:T(1024)S(1)}, u32[]{:S(2)}) copy-start(s32[1024]{0:T(1024)S(1)} %pad_clamp_fusion.2) | copy-start | bytes 12292
  76.7 5.8 %copy-start.29 = (s32[1024]{0:T(1024)}, s32[1024]{0:T(1024)S(1)}, u32[]{:S(2)}) copy-start(s32[1024]{0:T(1024)S(1)} %pad_clamp_fusion.1) | copy-start | bytes 12292
  76.8 5.7 %copy-start.52 = (pred[80]{0:T(512)(128)(4,1)S(1)}, pred[80]{0:T(512)(128)(4,1)}, u32[]{:S(2)}) copy-start(pred[80]{0:T(512)(128)(4,1)} %compare_and_fusion.2) | copy-start | bytes 244
  85.8 12.0 %all-to-all-start.1 = ((f32[80,16,22]{0,2,1:T(8,128)}), f32[80,16,22]{0,2,1:T(8,128)S(1)}, u32[]{:S(2)}, u32[]{:S(2)}) async-start(f32[80,16,22]{0,2,1:T(8,128)} %all_to_all.26), calls=%async_computation.1 | async-start | bytes 393216 | tf_op jit(solution)/shard_map/all_to_all | solution.py:258
  91.9 8.4 %copy-start.21 = (f32[4,16,16,1]{2,1,0,3:T(8,128)S(1)}, f32[4,16,16,1]{2,1,0,3:T(8,128)}, u32[]{:S(2)}) copy-start(f32[4,16,16,1]{2,1,0,3:T(8,128)} %constant.87) | copy-start | bytes 12292
  103.3 3.8 %copy-start.6 = (f32[5,16,6,128]{3,2,1,0:T(8,128)S(1)}, f32[5,16,6,128]{3,2,1,0:T(8,128)}, u32[]{:S(2)}) copy-start(f32[5,16,6,128]{3,2,1,0:T(8,128)} %copy-done.5) | copy-start | bytes 737284
  103.4 3.8 %copy-start.34 = (pred[768]{0:T(1024)(128)(4,1)S(1)}, pred[768]{0:T(1024)(128)(4,1)}, u32[]{:S(2)}) copy-start(pred[768]{0:T(1024)(128)(4,1)} %compare_and_fusion) | copy-start | bytes 2308
  106.0 4.1 %copy-start.17 = (f32[64,6,16,1]{0,2,1,3:T(8,128)S(1)}, f32[64,6,16,1]{0,2,1,3:T(8,128)}, u32[]{:S(2)}) copy-start(f32[64,6,16,1]{0,2,1,3:T(8,128)} %constant.88) | copy-start | bytes 73732
  107.2 4.2 %copy-start.12 = (f32[320,128]{1,0:T(8,128)S(1)}, f32[320,128]{1,0:T(8,128)}, u32[]{:S(2)}) copy-start(f32[320,128]{1,0:T(8,128)} %param.32) | copy-start | bytes 491524
  111.4 48.0 %copy-start.20 = (f32[6,16,64,1]{2,1,0,3:T(8,128)S(1)}, f32[6,16,64,1]{2,1,0,3:T(8,128)}, u32[]{:S(2)}) copy-start(f32[6,16,64,1]{2,1,0,3:T(8,128)} %constant.85) | copy-start | bytes 73732
  167.6 3.7 %copy-start.16 = (f32[3,64,64,1]{2,1,0,3:T(8,128)S(1)}, f32[3,64,64,1]{2,1,0,3:T(8,128)}, u32[]{:S(2)}) copy-start(f32[3,64,64,1]{2,1,0,3:T(8,128)} %constant.84) | copy-start | bytes 147460
  167.6 5.0 %copy-start.45 = (pred[16]{0:T(512)(128)(4,1)S(1)}, pred[16]{0:T(512)(128)(4,1)}, u32[]{:S(2)}) copy-start(pred[16]{0:T(512)(128)(4,1)} %copy-done.44) | copy-start | bytes 52
  167.6 5.0 %copy-start.47 = (pred[16]{0:T(512)(128)(4,1)S(1)}, pred[16]{0:T(512)(128)(4,1)}, u32[]{:S(2)}) copy-start(pred[16]{0:T(512)(128)(4,1)} %copy-done.46) | copy-start | bytes 52
  167.6 11.3 %copy-start.49 = (pred[16]{0:T(512)(128)(4,1)S(1)}, pred[16]{0:T(512)(128)(4,1)}, u32[]{:S(2)}) copy-start(pred[16]{0:T(512)(128)(4,1)} %copy-done.48) | copy-start | bytes 52
  167.6 11.3 %copy-start.51 = (pred[16]{0:T(512)(128)(4,1)S(1)}, pred[16]{0:T(512)(128)(4,1)}, u32[]{:S(2)}) copy-start(pred[16]{0:T(512)(128)(4,1)} %copy-done.50) | copy-start | bytes 52
  171.3 9.9 %copy-start.14 = (f32[352,80]{1,0:T(8,128)S(1)}, f32[352,80]{1,0:T(8,128)}, u32[]{:S(2)}) copy-start(f32[352,80]{1,0:T(8,128)} %gather_fusion.12) | copy-start | bytes 337924
  171.3 9.9 %copy-start.41 = (pred[352]{0:T(512)(128)(4,1)S(1)}, pred[352]{0:T(512)(128)(4,1)}, u32[]{:S(2)}) copy-start(pred[352]{0:T(512)(128)(4,1)} %copy-done.40) | copy-start | bytes 1060
  171.3 16.6 %copy-start.53 = (pred[80]{0:T(512)(128)(4,1)S(1)}, pred[80]{0:T(512)(128)(4,1)}, u32[]{:S(2)}) copy-start(pred[80]{0:T(512)(128)(4,1)} %compare_and_fusion.2) | copy-start | bytes 244
  171.3 16.7 %copy-start.30 = (s32[1024]{0:T(1024)S(1)}, s32[1024]{0:T(1024)}, u32[]{:S(2)}) copy-start(s32[1024]{0:T(1024)} %copy-done.29) | copy-start | bytes 12292
  172.6 16.5 %copy-start.43 = (pred[352]{0:T(512)(128)(4,1)S(1)}, pred[352]{0:T(512)(128)(4,1)}, u32[]{:S(2)}) copy-start(pred[352]{0:T(512)(128)(4,1)} %compare_and_fusion.1) | copy-start | bytes 1060
  172.9 17.1 %collective-permute-start.4 = (f32[1,1280]{1,0:T(1,128)S(1)}, f32[1,1280]{1,0:T(1,128)S(1)}, u32[]{:S(2)}, u32[]{:S(2)}) collective-permute-start(f32[1,1280]{1,0:T(1,128)S(1)} %slice.73), channel_id=1, source_target_pairs={{0,16},{1,17},{2,18},{3,19},{4,20},{5,21},{6,22},{7,23},{8,24},{9,... | collective-permute-start | bytes 15368 | tf_op jit(solution)/shard_map/ppermute | solution.py:19
  174.4 15.8 %collective-permute-start.5 = (f32[1,1280]{1,0:T(1,128)S(1)}, f32[1,1280]{1,0:T(1,128)S(1)}, u32[]{:S(2)}, u32[]{:S(2)}) collective-permute-start(f32[1,1280]{1,0:T(1,128)S(1)} %slice.74), channel_id=1, source_target_pairs={{16,0},{17,1},{18,2},{19,3},{20,4},{21,5},{22,6},{23,7},{24,8},{25... | collective-permute-start | bytes 15368 | tf_op jit(solution)/shard_map/ppermute | solution.py:20
  179.2 11.1 %collective-permute-start.6 = (f32[1,1280]{1,0:T(1,128)S(1)}, f32[1,1280]{1,0:T(1,128)S(1)}, u32[]{:S(2)}, u32[]{:S(2)}) collective-permute-start(f32[1,1280]{1,0:T(1,128)S(1)} %slice.75), channel_id=1, source_target_pairs={{0,1},{1,2},{2,3},{3,4},{4,5},{5,6},{6,7},{7,8},{8,9},{9,10},{10,1... | collective-permute-start | bytes 15368 | tf_op jit(solution)/shard_map/ppermute | solution.py:19
  179.5 11.1 %collective-permute-start.7 = (f32[1,1280]{1,0:T(1,128)S(1)}, f32[1,1280]{1,0:T(1,128)S(1)}, u32[]{:S(2)}, u32[]{:S(2)}) collective-permute-start(f32[1,1280]{1,0:T(1,128)S(1)} %slice.76), channel_id=1, source_target_pairs={{1,0},{2,1},{3,2},{4,3},{5,4},{6,5},{7,6},{8,7},{9,8},{10,9},{11,1... | collective-permute-start | bytes 15368 | tf_op jit(solution)/shard_map/ppermute | solution.py:20
  182.1 11.8 %all-to-all-start.2 = ((f32[80,16,22]{0,2,1:T(8,128)}), f32[80,16,22]{0,2,1:T(8,128)S(1)}, u32[]{:S(2)}, u32[]{:S(2)}) async-start(f32[80,16,22]{0,2,1:T(8,128)} %all_to_all.28), calls=%async_computation.2 | async-start | bytes 393216 | tf_op jit(solution)/shard_map/all_to_all | solution.py:257
  189.1 11.9 %copy-start.23 = (f32[4,16,16,1]{2,1,0,3:T(8,128)S(1)}, f32[4,16,16,1]{2,1,0,3:T(8,128)}, u32[]{:S(2)}) copy-start(f32[4,16,16,1]{2,1,0,3:T(8,128)} %constant.86) | copy-start | bytes 12292
  189.1 11.9 %copy-start.24 = (f32[4,352]{1,0:T(4,128)S(1)}, f32[4,352]{1,0:T(4,128)}, u32[]{:S(2)}) copy-start(f32[4,352]{1,0:T(4,128)} %fusion.27) | copy-start | bytes 16900
  193.8 12.5 %all-to-all-start.3 = ((f32[80,16,22]{0,2,1:T(8,128)}), f32[80,16,22]{0,2,1:T(8,128)S(1)}, u32[]{:S(2)}, u32[]{:S(2)}) async-start(f32[80,16,22]{0,2,1:T(8,128)} %all_to_all.30), calls=%async_computation.3 | async-start | bytes 393216 | tf_op jit(solution)/shard_map/all_to_all | solution.py:258
  200.4 6.6 %copy-start.22 = (f32[4,16,16,1]{2,1,0,3:T(8,128)S(1)}, f32[4,16,16,1]{2,1,0,3:T(8,128)}, u32[]{:S(2)}) copy-start(f32[4,16,16,1]{2,1,0,3:T(8,128)} %constant.87) | copy-start | bytes 12292
  200.8 6.9 %copy-start.26 = (s32[352]{0:T(512)S(1)}, s32[352]{0:T(512)}, u32[]{:S(2)}) copy-start(s32[352]{0:T(512)} %copy-done.25) | copy-start | bytes 4228
  201.1 7.0 %copy-start.28 = (s32[1024]{0:T(1024)S(1)}, s32[1024]{0:T(1024)}, u32[]{:S(2)}) copy-start(s32[1024]{0:T(1024)} %pad_clamp_fusion) | copy-start | bytes 12292
  (25 other events, 41.3 us)
where the time goes:
time: 265 us; the launch traced here: 264 us
  blocking collectives  124 us (47%)
  starting transfers between devices  41.6 us (16%)
  local copies, waits for them, and re-layouts  40.4 us (15%)
  matrix products  24.4 us (9%)
  other arithmetic  12.4 us (5%)
  between operations  10.7 us (4%)
  waiting for transfers between devices  10.2 us (4%)
    psum x3, blocking collectives, merged_global(): return lax.psum(partial_values, ('gx', 'yz'))  124 us
    all_to_all x2, starting transfers between devices, on_device(): lax.all_to_all(fine_send, 'yz', split_axis=1, concat_axis=1, tiled=True)  13.7 us
    all_to_all x2, starting transfers between devices, on_device(): lax.all_to_all(outgoing, 'yz', split_axis=1, concat_axis=1, tiled=True)  12.6 us
    ppermute x4, starting transfers between devices, with_halo(): after = lax.ppermute(leading, axis, down)  12.6 us
    dot_general x2, matrix products, jacobian(): jnp.einsum('dabe,bne->dane', flux_blocks, nodal_view, precision=maximum_d...  7.32 us
    all_to_all x2, waiting for transfers between devices, on_device(): lax.all_to_all(outgoing, 'yz', split_axis=1, concat_axis=1, tiled=True)  7.04 us
    gather x4, local copies, waits for them, and re-layouts, on_device(): jnp.take(trace_table, near_index, axis=1, mode='fill', fill_value=0.0)  5.46 us
  transfers between devices with their start and end apart: 12, of which 3 were waited for; matrix products, arithmetic and copies ran while one was open for 10% of the time, Pallas kernels for 0%

commit v1 on v0

--- a/solution.py
+++ b/solution.py
@@ -7,6 +7,18 @@
 ITERS = 2
 maximum_depth = lax.Precision.HIGHEST
 epsilon = 1e-06
+
+
+def split_up(x, dim, size):
+    lengths = x.shape
+    blocks = x.reshape(*lengths[:dim], size, lengths[dim] // size, *lengths[dim + 1 :])
+    return jnp.moveaxis(blocks, dim, 0)
+
+
+def joined_along(parts, dim):
+    lengths = list(parts.shape[1:])
+    lengths[dim] *= parts.shape[0]
+    return jnp.moveaxis(parts, 0, dim).reshape(lengths)
 
 
 def with_halo(shard, sides, width, wrap):
@@ -254,7 +266,18 @@
         )
         coarse = jnp.take(own_faces, coarse_mortar_table_slot[0], axis=1)
         outgoing = jnp.take(coarse, incoming_mortar_index[0], axis=1, mode="fill", fill_value=0.0)
-        fine_recv = lax.all_to_all(fine_send, "yz", split_axis=1, concat_axis=1, tiled=True)
+        length_2, place = (lax.axis_size("yz"), lax.axis_index("yz"))
+        blocks = split_up(fine_send, 1, length_2)
+        outs = [blocks[place]]
+        for step in range(1, length_2):
+            sent = blocks[(place + step) % length_2]
+            outs.append(
+                lax.ppermute(
+                    sent, "yz", [(i_2, (i_2 + step) % length_2) for i_2 in range(length_2)]
+                )
+            )
+        blocks = jnp.stack(outs)[(place - jnp.arange(length_2)) % length_2]
+        fine_recv = joined_along(blocks, 1)
         coarse_cols = lax.all_to_all(outgoing, "yz", split_axis=1, concat_axis=1, tiled=True)
         hang_sum = mortar_sums(
             fine_recv, incoming_mortar_index[0], incoming_quadrant_index[0], projection, hang_count

time: 265 us -> 297 us (1.12)
  starting transfers between devices: 41.6 us -> 73 us
  waiting for transfers between devices: 10.2 us -> 2.82 us
  local copies, waits for them, and re-layouts: 40.4 us -> 47.2 us
    ppermute x0 -> x30, starting transfers between devices: none -> 40.1 us  [on_device(): lax.ppermute(sent, 'yz', [(i_2, (i_2 + step) % length_2) for i_2 in range...]
    all_to_all x2 -> x0, starting transfers between devices: 13.7 us -> none  [on_device(): lax.all_to_all(fine_send, 'yz', split_axis=1, concat_axis=1, tiled=True)]
    all_to_all x2, waiting for transfers between devices: 7.04 us -> 0.01 us  [on_device(): lax.all_to_all(outgoing, 'yz', split_axis=1, concat_axis=1, tiled=True)]
    all_to_all x2, starting transfers between devices: 12.6 us -> 17.6 us  [on_device(): lax.all_to_all(outgoing, 'yz', split_axis=1, concat_axis=1, tiled=True)]
    all_to_all x4 -> x0, local copies, waits for them, and re-layouts: 3.84 us -> none  [on_device(): lax.all_to_all(fine_send, 'yz', split_axis=1, concat_axis=1, tiled=True)]
    all_to_all x2 -> x0, waiting for transfers between devices: 3.11 us -> none  [on_device(): lax.all_to_all(fine_send, 'yz', split_axis=1, concat_axis=1, tiled=True)]
  transfers between devices with their start and end apart: 12 -> 40, of which waited for: 3 -> 6; matrix products, arithmetic and copies ran while one was open for 10% -> 10% of each run, Pallas kernels for 0% -> 0%
where the time goes in v1:
time: 297 us; the launch traced here: 295 us
  blocking collectives  124 us (42%)
  starting transfers between devices  73 us (25%)
  local copies, waits for them, and re-layouts  47.2 us (16%)
  matrix products  23 us (8%)
  other arithmetic  12.5 us (4%)
  between operations  11.8 us (4%)
    psum x3, blocking collectives, merged_global(): return lax.psum(partial_values, ('gx', 'yz'))  124 us
    ppermute x30, starting transfers between devices, on_device(): lax.ppermute(sent, 'yz', [(i_2, (i_2 + step) % length_2) for i_2 in range...  40.1 us
    all_to_all x2, starting transfers between devices, on_device(): lax.all_to_all(outgoing, 'yz', split_axis=1, concat_axis=1, tiled=True)  17.6 us
    ppermute x4, starting transfers between devices, with_halo(): after = lax.ppermute(leading, axis, down)  12.7 us
    dot_general x2, matrix products, jacobian(): jnp.einsum('dabe,bne->dane', flux_blocks, nodal_view, precision=maximum_d...  7.31 us
  transfers between devices with their start and end apart: 40, of which 6 were waited for; matrix products, arithmetic and copies ran while one was open for 10% of the time, Pallas kernels for 0%

profile of v1, /device:TPU:14, one launch (start us, length us, event | category | flops | bytes accessed | tf_op | source)
XLA Modules:
  0.0 294.8 jit_solution(17781276768996939622)
XLA Ops:
  1.0 1.5 convolution_multiply_fusion
  2.6 2.2 multiply_reduce_fusion.3
  4.8 40.6 %psum.21 = f32[1]{0:T(128)} all-reduce(f32[1]{0:T(128)} %bitcast), channel_id=1, replica_groups=mesh['gx'=2,'yz'=16] {'gx','yz'}, use_global_device_ids=true, to_apply=%region_1.0 | all-reduce | flops 1 | bytes 8 | tf_op jit(solution)/shard_map/psum | solution.py:213
  49.0 1.3 collective-permute-start
  51.8 4.5 %collective-permute-start.1 = (f32[1,1280]{1,0:T(1,128)}, f32[1,1280]{1,0:T(1,128)S(1)}, u32[]{:S(2)}, u32[]{:S(2)}) collective-permute-start(f32[1,1280]{1,0:T(1,128)} %slice.66), channel_id=1, source_target_pairs={{16,0},{17,1},{18,2},{19,3},{20,4},{21,5},{22,6},{23,7},{24,8},{25... | collective-permute-start | bytes 15368 | tf_op jit(solution)/shard_map/ppermute | solution.py:32
  59.2 1.7 collective-permute-start.3
  67.8 9.2 %all-to-all-start = ((f32[80,16,22]{0,2,1:T(8,128)}), f32[80,16,22]{0,2,1:T(8,128)}, u32[]{:S(2)}, u32[]{:S(2)}) async-start(f32[80,16,22]{0,2,1:T(8,128)} %all_to_all.12), calls=%async_computation | async-start | bytes 393216 | tf_op jit(solution)/shard_map/all_to_all | solution.py:281
  79.4 3.7 %convolution_bitcast_fusion.1 = f32[3,5,64,128]{2,1,0,3:T(8,128)S(1)} fusion(f32[5,64,128,1]{1,0,3,2:T(8,128)} %copy.178, f32[3,5,5,128]{2,1,0,3:T(8,128)S(1)} %copy.128), kind=kOutput, calls=%fused_computation.19 | convolution fusion | flops 7372800 | bytes 693760 | tf_op jit(solution)/shard_map/dabe,bne->dane/dot_general | solution.py:129
  83.1 2.0 convolution_bitcast_fusion.13
  85.7 1.5 collective-permute-start.5
  88.4 1.5 collective-permute-start.7
  91.6 2.4 collective-permute-start.9
  94.7 1.8 collective-permute-start.10
  97.9 2.3 collective-permute-start.13
  100.2 2.8 collective-permute-start.14
  103.7 1.5 collective-permute-start.17
  105.2 2.3 collective-permute-start.18
  110.8 1.4 reshape.487
  113.1 2.1 copy.142
  115.2 1.4 reshape.489
  117.3 2.6 gather_fusion.9
  124.0 1.3 fusion.10
  125.9 1.2 fusion.17
  127.1 1.3 pad_maximum_fusion
  128.4 41.9 %psum.22 = f32[2]{0:T(128)S(1)} all-reduce(f32[2]{0:T(128)S(1)} %pad_maximum_fusion), channel_id=1, replica_groups=mesh['gx'=2,'yz'=16] {'gx','yz'}, use_global_device_ids=true, to_apply=%region_6.12 | all-reduce | flops 2 | bytes 16 | tf_op jit(solution)/shard_map/psum | solution.py:213
  177.6 1.6 gather_fusion.14
  179.2 1.7 select_bitcast_fusion.1
  180.9 1.6 reshape.284
  182.6 1.3 constant_dynamic-update-slice_fusion.37
  183.9 1.5 dynamic-slice_bitcast_fusion
  187.9 3.7 %convolution_bitcast_fusion = f32[3,5,64,128]{2,1,0,3:T(8,128)S(1)} fusion(f32[5,64,128,1]{1,0,3,2:T(8,128)} %copy.185, f32[3,5,5,128]{2,1,0,3:T(8,128)S(1)} %copy.128), kind=kOutput, calls=%fused_computation.18 | convolution fusion | flops 7372800 | bytes 693760 | tf_op jit(solution)/shard_map/dabe,bne->dane/dot_general | solution.py:129
  191.6 1.3 convolution_bitcast_fusion.10
  193.2 1.3 collective-permute-start.19
  194.8 4.7 %collective-permute-start.20 = (f32[1,1280]{1,0:T(1,128)S(1)}, f32[1,1280]{1,0:T(1,128)S(1)}, u32[]{:S(2)}, u32[]{:S(2)}) collective-permute-start(f32[1,1280]{1,0:T(1,128)S(1)} %slice.74), channel_id=1, source_target_pairs={{16,0},{17,1},{18,2},{19,3},{20,4},{21,5},{22,6},{23,7},{24,8},{25... | collective-permute-start | bytes 15368 | tf_op jit(solution)/shard_map/ppermute | solution.py:32
  200.1 1.8 collective-permute-start.22
  203.9 8.4 %all-to-all-start.1 = ((f32[80,16,22]{0,2,1:T(8,128)}), f32[80,16,22]{0,2,1:T(8,128)S(1)}, u32[]{:S(2)}, u32[]{:S(2)}) async-start(f32[80,16,22]{0,2,1:T(8,128)} %all_to_all.14), calls=%async_computation.1 | async-start | bytes 393216 | tf_op jit(solution)/shard_map/all_to_all | solution.py:281
  212.3 1.5 collective-permute-start.24
  215.1 1.5 collective-permute-start.26
  217.8 2.4 collective-permute-start.28
  220.3 1.9 collective-permute-start.29
  223.5 2.3 collective-permute-start.32
  225.8 2.8 collective-permute-start.33
  229.3 1.5 collective-permute-start.36
  230.8 2.3 collective-permute-start.37
  238.4 1.6 gather_fusion.17
  241.8 1.2 fusion.20
  243.0 2.1 pad_maximum_fusion.1
  245.1 41.9 %psum.23 = f32[3]{0:T(128)S(1)} all-reduce(f32[3]{0:T(128)S(1)} %pad_maximum_fusion.1), channel_id=1, replica_groups=mesh['gx'=2,'yz'=16] {'gx','yz'}, use_global_device_ids=true, to_apply=%region_12.18 | all-reduce | flops 3 | bytes 24 | tf_op jit(solution)/shard_map/psum | solution.py:213
  (407 shorter events, 55.3 us)
Async XLA Ops:
  0.0 46.1 %copy-start.19 = (f32[6,16,64,1]{2,1,0,3:T(8,128)S(1)}, f32[6,16,64,1]{2,1,0,3:T(8,128)}, u32[]{:S(2)}) copy-start(f32[6,16,64,1]{2,1,0,3:T(8,128)} %constant.231) | copy-start | bytes 73732
  2.6 44.9 %copy-start.82 = (s32[1,2,16]{2,1,0:T(2,128)S(1)}, s32[1,2,16]{2,1,0:T(2,128)}, u32[]{:S(2)}) copy-start(s32[1,2,16]{2,1,0:T(2,128)} %param.40) | copy-start | bytes 388
  2.6 44.9 %copy-start.83 = (s32[1,2,16]{2,1,0:T(2,128)S(1)}, s32[1,2,16]{2,1,0:T(2,128)}, u32[]{:S(2)}) copy-start(s32[1,2,16]{2,1,0:T(2,128)} %param.39) | copy-start | bytes 388
  46.1 79.7 %copy-start.3 = (f32[128,320]{0,1:T(8,128)}, f32[128,320]{0,1:T(8,128)S(1)}, u32[]{:S(2)}) copy-start(f32[128,320]{0,1:T(8,128)S(1)} %broadcast_divide_fusion) | copy-start | bytes 491524
  49.0 36.7 %collective-permute-start = (f32[1,1280]{1,0:T(1,128)}, f32[1,1280]{1,0:T(1,128)S(1)}, u32[]{:S(2)}, u32[]{:S(2)}) collective-permute-start(f32[1,1280]{1,0:T(1,128)} %slice.64), channel_id=1, source_target_pairs={{0,16},{1,17},{2,18},{3,19},{4,20},{5,21},{6,22},{7,23},{8,24},{9,... | collective-permute-start | bytes 15368 | tf_op jit(solution)/shard_map/ppermute | solution.py:31
  51.8 35.5 %collective-permute-start.1 = (f32[1,1280]{1,0:T(1,128)}, f32[1,1280]{1,0:T(1,128)S(1)}, u32[]{:S(2)}, u32[]{:S(2)}) collective-permute-start(f32[1,1280]{1,0:T(1,128)} %slice.66), channel_id=1, source_target_pairs={{16,0},{17,1},{18,2},{19,3},{20,4},{21,5},{22,6},{23,7},{24,8},{25... | collective-permute-start | bytes 15368 | tf_op jit(solution)/shard_map/ppermute | solution.py:32
  57.8 30.7 %collective-permute-start.2 = (f32[1,1280]{1,0:T(1,128)}, f32[1,1280]{1,0:T(1,128)S(1)}, u32[]{:S(2)}, u32[]{:S(2)}) collective-permute-start(f32[1,1280]{1,0:T(1,128)} %slice.68), channel_id=1, source_target_pairs={{0,1},{1,2},{2,3},{3,4},{4,5},{5,6},{6,7},{7,8},{8,9},{9,10},{10,1... | collective-permute-start | bytes 15368 | tf_op jit(solution)/shard_map/ppermute | solution.py:31
  59.2 30.9 %collective-permute-start.3 = (f32[1,1280]{1,0:T(1,128)}, f32[1,1280]{1,0:T(1,128)}, u32[]{:S(2)}, u32[]{:S(2)}) collective-permute-start(f32[1,1280]{1,0:T(1,128)} %slice.70), channel_id=1, source_target_pairs={{1,0},{2,1},{3,2},{4,3},{5,4},{6,5},{7,6},{8,7},{9,8},{10,9},{11,1... | collective-permute-start | bytes 15368 | tf_op jit(solution)/shard_map/ppermute | solution.py:32
  64.5 27.1 %collective-permute-start.4 = (f32[80,22]{0,1:T(8,128)}, f32[80,22]{0,1:T(8,128)}, u32[]{:S(2)}, u32[]{:S(2)}) collective-permute-start(f32[80,22]{0,1:T(8,128)} %get-tuple-element.52), channel_id=1, source_target_pairs={{0,1},{1,2},{2,3},{3,4},{4,5},{5,6},{6,7},{7,8},{8,9},{9,10},{10,1... | collective-permute-start | bytes 21128 | tf_op jit(solution)/shard_map/ppermute | solution.py:275
  65.1 47.6 %copy-start.27 = (s32[352]{0:T(512)}, s32[352]{0:T(512)S(1)}, u32[]{:S(2)}) copy-start(s32[352]{0:T(512)S(1)} %reduce.7) | copy-start | bytes 4228
  67.8 45.3 %all-to-all-start = ((f32[80,16,22]{0,2,1:T(8,128)}), f32[80,16,22]{0,2,1:T(8,128)}, u32[]{:S(2)}, u32[]{:S(2)}) async-start(f32[80,16,22]{0,2,1:T(8,128)} %all_to_all.12), calls=%async_computation | async-start | bytes 393216 | tf_op jit(solution)/shard_map/all_to_all | solution.py:281
  79.3 32.9 %copy-start.25 = (f32[4,352]{1,0:T(4,128)}, f32[4,352]{1,0:T(4,128)S(1)}, u32[]{:S(2)}) copy-start(f32[4,352]{1,0:T(4,128)S(1)} %fusion.27) | copy-start | bytes 16900
  85.7 9.0 %collective-permute-start.5 = (f32[80,22]{0,1:T(8,128)}, f32[80,22]{0,1:T(8,128)S(1)}, u32[]{:S(2)}, u32[]{:S(2)}) collective-permute-start(f32[80,22]{0,1:T(8,128)} %get-tuple-element.51), channel_id=1, source_target_pairs={{0,2},{1,3},{2,4},{3,5},{4,6},{5,7},{6,8},{7,9},{8,10},{9,11},{10,... | collective-permute-start | bytes 21128 | tf_op jit(solution)/shard_map/ppermute | solution.py:275
  87.3 9.2 %collective-permute-start.6 = (f32[80,22]{0,1:T(8,128)}, f32[80,22]{0,1:T(8,128)S(1)}, u32[]{:S(2)}, u32[]{:S(2)}) collective-permute-start(f32[80,22]{0,1:T(8,128)} %get-tuple-element.50), channel_id=1, source_target_pairs={{0,3},{1,4},{2,5},{3,6},{4,7},{5,8},{6,9},{7,10},{8,11},{9,12},{10... | collective-permute-start | bytes 21128 | tf_op jit(solution)/shard_map/ppermute | solution.py:275
  88.4 8.8 %collective-permute-start.7 = (f32[80,22]{0,1:T(8,128)S(1)}, f32[80,22]{0,1:T(8,128)S(1)}, u32[]{:S(2)}, u32[]{:S(2)}) collective-permute-start(f32[80,22]{0,1:T(8,128)S(1)} %copy-done.57), channel_id=1, source_target_pairs={{0,4},{1,5},{2,6},{3,7},{4,8},{5,9},{6,10},{7,11},{8,12},{9,13},{1... | collective-permute-start | bytes 21128 | tf_op jit(solution)/shard_map/ppermute | solution.py:275
  90.1 7.8 %collective-permute-start.8 = (f32[80,22]{0,1:T(8,128)S(1)}, f32[80,22]{0,1:T(8,128)S(1)}, u32[]{:S(2)}, u32[]{:S(2)}) collective-permute-start(f32[80,22]{0,1:T(8,128)S(1)} %copy-done.56), channel_id=1, source_target_pairs={{0,5},{1,6},{2,7},{3,8},{4,9},{5,10},{6,11},{7,12},{8,13},{9,14},{... | collective-permute-start | bytes 21128 | tf_op jit(solution)/shard_map/ppermute | solution.py:275
  91.6 8.6 %collective-permute-start.9 = (f32[80,22]{0,1:T(8,128)S(1)}, f32[80,22]{0,1:T(8,128)S(1)}, u32[]{:S(2)}, u32[]{:S(2)}) collective-permute-start(f32[80,22]{0,1:T(8,128)S(1)} %copy-done.54), channel_id=1, source_target_pairs={{0,6},{1,7},{2,8},{3,9},{4,10},{5,11},{6,12},{7,13},{8,14},{9,15},... | collective-permute-start | bytes 21128 | tf_op jit(solution)/shard_map/ppermute | solution.py:275
  94.7 8.3 %collective-permute-start.10 = (f32[80,22]{0,1:T(8,128)S(1)}, f32[80,22]{0,1:T(8,128)S(1)}, u32[]{:S(2)}, u32[]{:S(2)}) collective-permute-start(f32[80,22]{0,1:T(8,128)S(1)} %copy-done.52), channel_id=1, source_target_pairs={{0,7},{1,8},{2,9},{3,10},{4,11},{5,12},{6,13},{7,14},{8,15},{9,0},... | collective-permute-start | bytes 21128 | tf_op jit(solution)/shard_map/ppermute | solution.py:275
  96.5 7.1 %collective-permute-start.11 = (f32[80,22]{0,1:T(8,128)S(1)}, f32[80,22]{0,1:T(8,128)S(1)}, u32[]{:S(2)}, u32[]{:S(2)}) collective-permute-start(f32[80,22]{0,1:T(8,128)S(1)} %copy-done.50), channel_id=1, source_target_pairs={{0,8},{1,9},{2,10},{3,11},{4,12},{5,13},{6,14},{7,15},{8,0},{9,1},... | collective-permute-start | bytes 21128 | tf_op jit(solution)/shard_map/ppermute | solution.py:275
  97.2 6.5 %collective-permute-start.12 = (f32[80,22]{0,1:T(8,128)S(1)}, f32[80,22]{0,1:T(8,128)S(1)}, u32[]{:S(2)}, u32[]{:S(2)}) collective-permute-start(f32[80,22]{0,1:T(8,128)S(1)} %copy-done.48), channel_id=1, source_target_pairs={{0,9},{1,10},{2,11},{3,12},{4,13},{5,14},{6,15},{7,0},{8,1},{9,2},... | collective-permute-start | bytes 21128 | tf_op jit(solution)/shard_map/ppermute | solution.py:275
  97.9 7.4 %collective-permute-start.13 = (f32[80,22]{0,1:T(8,128)S(1)}, f32[80,22]{0,1:T(8,128)S(1)}, u32[]{:S(2)}, u32[]{:S(2)}) collective-permute-start(f32[80,22]{0,1:T(8,128)S(1)} %copy-done.46), channel_id=1, source_target_pairs={{0,10},{1,11},{2,12},{3,13},{4,14},{5,15},{6,0},{7,1},{8,2},{9,3},... | collective-permute-start | bytes 21128 | tf_op jit(solution)/shard_map/ppermute | solution.py:275
  100.2 7.3 %collective-permute-start.14 = (f32[80,22]{0,1:T(8,128)S(1)}, f32[80,22]{0,1:T(8,128)S(1)}, u32[]{:S(2)}, u32[]{:S(2)}) collective-permute-start(f32[80,22]{0,1:T(8,128)S(1)} %copy-done.44), channel_id=1, source_target_pairs={{0,11},{1,12},{2,13},{3,14},{4,15},{5,0},{6,1},{7,2},{8,3},{9,4},{... | collective-permute-start | bytes 21128 | tf_op jit(solution)/shard_map/ppermute | solution.py:275
  103.0 4.5 %collective-permute-start.15 = (f32[80,22]{0,1:T(8,128)S(1)}, f32[80,22]{0,1:T(8,128)S(1)}, u32[]{:S(2)}, u32[]{:S(2)}) collective-permute-start(f32[80,22]{0,1:T(8,128)S(1)} %copy-done.42), channel_id=1, source_target_pairs={{0,12},{1,13},{2,14},{3,15},{4,0},{5,1},{6,2},{7,3},{8,4},{9,5},{1... | collective-permute-start | bytes 21128 | tf_op jit(solution)/shard_map/ppermute | solution.py:275
  103.6 4.1 %collective-permute-start.16 = (f32[80,22]{0,1:T(8,128)S(1)}, f32[80,22]{0,1:T(8,128)S(1)}, u32[]{:S(2)}, u32[]{:S(2)}) collective-permute-start(f32[80,22]{0,1:T(8,128)S(1)} %get-tuple-element.40), channel_id=1, source_target_pairs={{0,13},{1,14},{2,15},{3,0},{4,1},{5,2},{6,3},{7,4},{8,5},{9,6},{10... | collective-permute-start | bytes 21128 | tf_op jit(solution)/shard_map/ppermute | solution.py:275
  103.7 4.6 %collective-permute-start.17 = (f32[80,22]{0,1:T(8,128)S(1)}, f32[80,22]{0,1:T(8,128)S(1)}, u32[]{:S(2)}, u32[]{:S(2)}) collective-permute-start(f32[80,22]{0,1:T(8,128)S(1)} %get-tuple-element.39), channel_id=1, source_target_pairs={{0,14},{1,15},{2,0},{3,1},{4,2},{5,3},{6,4},{7,5},{8,6},{9,7},{10,... | collective-permute-start | bytes 21128 | tf_op jit(solution)/shard_map/ppermute | solution.py:275
  105.2 3.7 %collective-permute-start.18 = (f32[80,22]{0,1:T(8,128)S(1)}, f32[80,22]{0,1:T(8,128)S(1)}, u32[]{:S(2)}, u32[]{:S(2)}) collective-permute-start(f32[80,22]{0,1:T(8,128)S(1)} %get-tuple-element.38), channel_id=1, source_target_pairs={{0,15},{1,0},{2,1},{3,2},{4,3},{5,4},{6,5},{7,6},{8,7},{9,8},{10,9... | collective-permute-start | bytes 21128 | tf_op jit(solution)/shard_map/ppermute | solution.py:275
  125.2 48.2 %copy-start.20 = (f32[6,16,64,1]{2,1,0,3:T(8,128)S(1)}, f32[6,16,64,1]{2,1,0,3:T(8,128)}, u32[]{:S(2)}) copy-start(f32[6,16,64,1]{2,1,0,3:T(8,128)} %constant.231) | copy-start | bytes 73732
  193.2 19.1 %collective-permute-start.19 = (f32[1,1280]{1,0:T(1,128)S(1)}, f32[1,1280]{1,0:T(1,128)S(1)}, u32[]{:S(2)}, u32[]{:S(2)}) collective-permute-start(f32[1,1280]{1,0:T(1,128)S(1)} %slice.73), channel_id=1, source_target_pairs={{0,16},{1,17},{2,18},{3,19},{4,20},{5,21},{6,22},{7,23},{8,24},{9,... | collective-permute-start | bytes 15368 | tf_op jit(solution)/shard_map/ppermute | solution.py:31
  194.8 19.2 %collective-permute-start.20 = (f32[1,1280]{1,0:T(1,128)S(1)}, f32[1,1280]{1,0:T(1,128)S(1)}, u32[]{:S(2)}, u32[]{:S(2)}) collective-permute-start(f32[1,1280]{1,0:T(1,128)S(1)} %slice.74), channel_id=1, source_target_pairs={{16,0},{17,1},{18,2},{19,3},{20,4},{21,5},{22,6},{23,7},{24,8},{25... | collective-permute-start | bytes 15368 | tf_op jit(solution)/shard_map/ppermute | solution.py:32
  199.7 29.5 %copy-start.36 = (f32[80,22]{0,1:T(8,128)S(1)}, f32[80,22]{0,1:T(8,128)}, u32[]{:S(2)}) copy-start(f32[80,22]{0,1:T(8,128)} %get-tuple-element.25) | copy-start | bytes 21124
  199.7 15.4 %collective-permute-start.21 = (f32[1,1280]{1,0:T(1,128)S(1)}, f32[1,1280]{1,0:T(1,128)S(1)}, u32[]{:S(2)}, u32[]{:S(2)}) collective-permute-start(f32[1,1280]{1,0:T(1,128)S(1)} %slice.75), channel_id=1, source_target_pairs={{0,1},{1,2},{2,3},{3,4},{4,5},{5,6},{6,7},{7,8},{8,9},{9,10},{10,1... | collective-permute-start | bytes 15368 | tf_op jit(solution)/shard_map/ppermute | solution.py:31
  200.1 16.7 %collective-permute-start.22 = (f32[1,1280]{1,0:T(1,128)S(1)}, f32[1,1280]{1,0:T(1,128)S(1)}, u32[]{:S(2)}, u32[]{:S(2)}) collective-permute-start(f32[1,1280]{1,0:T(1,128)S(1)} %slice.76), channel_id=1, source_target_pairs={{1,0},{2,1},{3,2},{4,3},{5,4},{6,5},{7,6},{8,7},{9,8},{10,9},{11,1... | collective-permute-start | bytes 15368 | tf_op jit(solution)/shard_map/ppermute | solution.py:32
  201.9 15.9 %collective-permute-start.23 = (f32[80,22]{0,1:T(8,128)S(1)}, f32[80,22]{0,1:T(8,128)S(1)}, u32[]{:S(2)}, u32[]{:S(2)}) collective-permute-start(f32[80,22]{0,1:T(8,128)S(1)} %copy-done.55), channel_id=1, source_target_pairs={{0,1},{1,2},{2,3},{3,4},{4,5},{5,6},{6,7},{7,8},{8,9},{9,10},{10,1... | collective-permute-start | bytes 21128 | tf_op jit(solution)/shard_map/ppermute | solution.py:275
  203.9 33.1 %all-to-all-start.1 = ((f32[80,16,22]{0,2,1:T(8,128)}), f32[80,16,22]{0,2,1:T(8,128)S(1)}, u32[]{:S(2)}, u32[]{:S(2)}) async-start(f32[80,16,22]{0,2,1:T(8,128)} %all_to_all.14), calls=%async_computation.1 | async-start | bytes 393216 | tf_op jit(solution)/shard_map/all_to_all | solution.py:281
  212.3 7.9 %collective-permute-start.24 = (f32[80,22]{0,1:T(8,128)S(1)}, f32[80,22]{0,1:T(8,128)S(1)}, u32[]{:S(2)}, u32[]{:S(2)}) collective-permute-start(f32[80,22]{0,1:T(8,128)S(1)} %copy-done.53), channel_id=1, source_target_pairs={{0,2},{1,3},{2,4},{3,5},{4,6},{5,7},{6,8},{7,9},{8,10},{9,11},{10,... | collective-permute-start | bytes 21128 | tf_op jit(solution)/shard_map/ppermute | solution.py:275
  214.0 8.1 %collective-permute-start.25 = (f32[80,22]{0,1:T(8,128)S(1)}, f32[80,22]{0,1:T(8,128)S(1)}, u32[]{:S(2)}, u32[]{:S(2)}) collective-permute-start(f32[80,22]{0,1:T(8,128)S(1)} %copy-done.51), channel_id=1, source_target_pairs={{0,3},{1,4},{2,5},{3,6},{4,7},{5,8},{6,9},{7,10},{8,11},{9,12},{10... | collective-permute-start | bytes 21128 | tf_op jit(solution)/shard_map/ppermute | solution.py:275
  215.1 7.6 %collective-permute-start.26 = (f32[80,22]{0,1:T(8,128)S(1)}, f32[80,22]{0,1:T(8,128)S(1)}, u32[]{:S(2)}, u32[]{:S(2)}) collective-permute-start(f32[80,22]{0,1:T(8,128)S(1)} %copy-done.49), channel_id=1, source_target_pairs={{0,4},{1,5},{2,6},{3,7},{4,8},{5,9},{6,10},{7,11},{8,12},{9,13},{1... | collective-permute-start | bytes 21128 | tf_op jit(solution)/shard_map/ppermute | solution.py:275
  216.8 6.7 %collective-permute-start.27 = (f32[80,22]{0,1:T(8,128)S(1)}, f32[80,22]{0,1:T(8,128)S(1)}, u32[]{:S(2)}, u32[]{:S(2)}) collective-permute-start(f32[80,22]{0,1:T(8,128)S(1)} %copy-done.47), channel_id=1, source_target_pairs={{0,5},{1,6},{2,7},{3,8},{4,9},{5,10},{6,11},{7,12},{8,13},{9,14},{... | collective-permute-start | bytes 21128 | tf_op jit(solution)/shard_map/ppermute | solution.py:275
  217.8 8.0 %collective-permute-start.28 = (f32[80,22]{0,1:T(8,128)S(1)}, f32[80,22]{0,1:T(8,128)S(1)}, u32[]{:S(2)}, u32[]{:S(2)}) collective-permute-start(f32[80,22]{0,1:T(8,128)S(1)} %copy-done.45), channel_id=1, source_target_pairs={{0,6},{1,7},{2,8},{3,9},{4,10},{5,11},{6,12},{7,13},{8,14},{9,15},... | collective-permute-start | bytes 21128 | tf_op jit(solution)/shard_map/ppermute | solution.py:275
  220.3 8.3 %collective-permute-start.29 = (f32[80,22]{0,1:T(8,128)S(1)}, f32[80,22]{0,1:T(8,128)S(1)}, u32[]{:S(2)}, u32[]{:S(2)}) collective-permute-start(f32[80,22]{0,1:T(8,128)S(1)} %copy-done.43), channel_id=1, source_target_pairs={{0,7},{1,8},{2,9},{3,10},{4,11},{5,12},{6,13},{7,14},{8,15},{9,0},... | collective-permute-start | bytes 21128 | tf_op jit(solution)/shard_map/ppermute | solution.py:275
  222.1 7.1 %collective-permute-start.30 = (f32[80,22]{0,1:T(8,128)S(1)}, f32[80,22]{0,1:T(8,128)S(1)}, u32[]{:S(2)}, u32[]{:S(2)}) collective-permute-start(f32[80,22]{0,1:T(8,128)S(1)} %copy-done.41), channel_id=1, source_target_pairs={{0,8},{1,9},{2,10},{3,11},{4,12},{5,13},{6,14},{7,15},{8,0},{9,1},... | collective-permute-start | bytes 21128 | tf_op jit(solution)/shard_map/ppermute | solution.py:275
  222.8 6.5 %collective-permute-start.31 = (f32[80,22]{0,1:T(8,128)S(1)}, f32[80,22]{0,1:T(8,128)S(1)}, u32[]{:S(2)}, u32[]{:S(2)}) collective-permute-start(f32[80,22]{0,1:T(8,128)S(1)} %copy-done.40), channel_id=1, source_target_pairs={{0,9},{1,10},{2,11},{3,12},{4,13},{5,14},{6,15},{7,0},{8,1},{9,2},... | collective-permute-start | bytes 21128 | tf_op jit(solution)/shard_map/ppermute | solution.py:275
  223.5 7.4 %collective-permute-start.32 = (f32[80,22]{0,1:T(8,128)S(1)}, f32[80,22]{0,1:T(8,128)S(1)}, u32[]{:S(2)}, u32[]{:S(2)}) collective-permute-start(f32[80,22]{0,1:T(8,128)S(1)} %copy-done.39), channel_id=1, source_target_pairs={{0,10},{1,11},{2,12},{3,13},{4,14},{5,15},{6,0},{7,1},{8,2},{9,3},... | collective-permute-start | bytes 21128 | tf_op jit(solution)/shard_map/ppermute | solution.py:275
  225.8 7.3 %collective-permute-start.33 = (f32[80,22]{0,1:T(8,128)S(1)}, f32[80,22]{0,1:T(8,128)S(1)}, u32[]{:S(2)}, u32[]{:S(2)}) collective-permute-start(f32[80,22]{0,1:T(8,128)S(1)} %copy-done.38), channel_id=1, source_target_pairs={{0,11},{1,12},{2,13},{3,14},{4,15},{5,0},{6,1},{7,2},{8,3},{9,4},{... | collective-permute-start | bytes 21128 | tf_op jit(solution)/shard_map/ppermute | solution.py:275
  228.6 4.5 %collective-permute-start.34 = (f32[80,22]{0,1:T(8,128)S(1)}, f32[80,22]{0,1:T(8,128)S(1)}, u32[]{:S(2)}, u32[]{:S(2)}) collective-permute-start(f32[80,22]{0,1:T(8,128)S(1)} %copy-done.37), channel_id=1, source_target_pairs={{0,12},{1,13},{2,14},{3,15},{4,0},{5,1},{6,2},{7,3},{8,4},{9,5},{1... | collective-permute-start | bytes 21128 | tf_op jit(solution)/shard_map/ppermute | solution.py:275
  229.2 4.1 %collective-permute-start.35 = (f32[80,22]{0,1:T(8,128)S(1)}, f32[80,22]{0,1:T(8,128)S(1)}, u32[]{:S(2)}, u32[]{:S(2)}) collective-permute-start(f32[80,22]{0,1:T(8,128)S(1)} %copy-done.36), channel_id=1, source_target_pairs={{0,13},{1,14},{2,15},{3,0},{4,1},{5,2},{6,3},{7,4},{8,5},{9,6},{10... | collective-permute-start | bytes 21128 | tf_op jit(solution)/shard_map/ppermute | solution.py:275
  229.3 4.6 %collective-permute-start.36 = (f32[80,22]{0,1:T(8,128)S(1)}, f32[80,22]{0,1:T(8,128)S(1)}, u32[]{:S(2)}, u32[]{:S(2)}) collective-permute-start(f32[80,22]{0,1:T(8,128)S(1)} %get-tuple-element.24), channel_id=1, source_target_pairs={{0,14},{1,15},{2,0},{3,1},{4,2},{5,3},{6,4},{7,5},{8,6},{9,7},{10,... | collective-permute-start | bytes 21128 | tf_op jit(solution)/shard_map/ppermute | solution.py:275
  230.8 3.7 %collective-permute-start.37 = (f32[80,22]{0,1:T(8,128)S(1)}, f32[80,22]{0,1:T(8,128)S(1)}, u32[]{:S(2)}, u32[]{:S(2)}) collective-permute-start(f32[80,22]{0,1:T(8,128)S(1)} %get-tuple-element.23), channel_id=1, source_target_pairs={{0,15},{1,0},{2,1},{3,2},{4,3},{5,4},{6,5},{7,6},{8,7},{9,8},{10,9... | collective-permute-start | bytes 21128 | tf_op jit(solution)/shard_map/ppermute | solution.py:275
  (77 other events, 701.8 us)
